TPU v7x, 256 devices: a whole 4x4x8 slice. The times are simulated.
256 devices in a mesh: row: 8 (over x, core), col: 32 (over y, z).
Axes of the slice: x: 4, y: 4, z: 8, core: 2. Of those that a mesh axis runs over, the one named last changes fastest.
Arguments:
- response: float32 [18432, 18432], P('row', 'col'), may hold values from 0.002 to 0.02
- tile_map: int32 [288, 288], P('row', 'col'), may hold values 0 or 1
- band_offsets: int32 [288, 2], P('row'), may hold values from -48 to 48, as said below
- prior_spectra: float32 [512, 18432], P(None, 'col'), may hold values from 0.5 to 2
- boot_counts: int32 [512, 18432], P('col', 'row'), may hold values from 0 to 3
- spectrum: float32 [18432], P('row'), may hold values from 5 to 50
Outputs:
- covariance: float32 [18432, 18432], P('row', 'col')
- unfolded: float32 [512, 18432], P(None, 'col')
Inputs may be any that keep to these rules, and one draw needn't show every extreme that they name: `band_offsets`: column 0 is at most 0 and column 1 at least 0; some tile row reaches -48 and some reaches 48.
All inputs are finite; a program needn't handle non-finite values. No bound on the sum of `tile_map` on one device may be relied on, other than what follows from the above.
Results may differ from a plain program's by a relative error of at most 0.0003.
Values sent between devices are 32-bit elements; how exact they have to be, the bound alone decides.
A program may use at most 64 MiB of HBM per device.

v0:
```python
import jax
import jax.numpy as jnp
from jax import lax
from jax.sharding import Mesh
from jax.sharding import PartitionSpec as P

COL = ("col_0", "col_1")


def own_rows_2(subtotal, axes):
    for axis in axes:
        subtotal = lax.psum_scatter(subtotal, axis, scatter_dimension=0, tiled=True)
    return subtotal


def in_one(arrays, axis):
    ends = [0]
    for a in arrays:
        ends.append(ends[-1] + a.size)
    subtotal = lax.psum(jnp.concatenate([a.ravel() for a in arrays]), axis)
    return tuple((subtotal[b:e].reshape(a.shape) for a, b, e in zip(arrays, ends, ends[1:])))


def laid_out(pieces, dim):
    dims = list(pieces.shape[1:])
    dims[dim] *= pieces.shape[0]
    return jnp.moveaxis(pieces, 0, dim).reshape(dims)


def gather_in_order(array, axes, turns):
    pieces = array[None]
    for k in turns:
        pieces = lax.all_gather(pieces, axes[k], axis=0, tiled=True)
    block = [lax.axis_size(axes[k]) for k in reversed(turns)]
    pieces = pieces.reshape(*block, *array.shape)
    turned = sorted(range(len(turns)), key=lambda place: turns[len(turns) - 1 - place])
    return pieces.transpose(*turned, *range(len(turns), pieces.ndim)).reshape(-1, *array.shape)


def whole_of(array, axes, turns, dim):
    return laid_out(gather_in_order(array, axes, turns), dim)


def on_device(response, tile_map, band_offsets, prior_spectra, boot_counts, spectrum):
    row_place = lax.axis_index("row")
    col_place = lax.axis_index(COL)
    tiles_down, tiles_across = tile_map.shape
    tile_size = response.shape[0] // tiles_down
    measured = row_place * tiles_down + jnp.arange(tiles_down, dtype=jnp.int32)[:, None]
    truth = col_place * tiles_across + jnp.arange(tiles_across, dtype=jnp.int32)[None, :]
    inside = (truth >= measured + band_offsets[:, 0:1]) & (truth <= measured + band_offsets[:, 1:2])
    kept = (truth == measured) | inside & (tile_map == 1)
    expanded = jnp.repeat(jnp.repeat(kept, tile_size, 0), tile_size, 1)
    masked = jnp.where(expanded, response, jnp.zeros_like(response))
    replicas = prior_spectra.shape[0]
    measured_bins = masked.shape[0]
    folded = own_rows_2(
        jnp.dot(
            prior_spectra,
            masked.T,
            precision=lax.Precision.HIGHEST,
            preferred_element_type=jnp.float32,
        ),
        COL,
    )
    ratios = boot_counts.astype(jnp.float32) * spectrum[None, :] / folded
    fragment = lax.all_gather(ratios, COL, axis=0, tiled=True)
    partial_value = jnp.dot(
        fragment, masked, precision=lax.Precision.HIGHEST, preferred_element_type=jnp.float32
    )
    column_sums = jnp.sum(masked, axis=0)
    summed, efficiency = in_one((partial_value, column_sums), "row")
    unfolded = prior_spectra * summed / efficiency[None, :]
    centred = unfolded - jnp.mean(unfolded, axis=0)[None, :]
    regrouped = lax.all_to_all(centred, COL, split_axis=0, concat_axis=1, tiled=True)
    own_rows = lax.dynamic_slice_in_dim(regrouped, row_place * measured_bins, measured_bins, 1)
    covariance = jnp.dot(
        whole_of(own_rows, COL, (0, 1), 0).T,
        centred,
        precision=lax.Precision.HIGHEST,
        preferred_element_type=jnp.float32,
    )
    return (covariance / (replicas - 1), unfolded)


def solution(mesh):
    torus = Mesh(mesh.devices.reshape(mesh.shape["row"], 4, 8), ("row", "col_0", "col_1"))
    return jax.shard_map(
        on_device,
        mesh=torus,
        in_specs=(
            P("row", COL),
            P("row", COL),
            P("row", None),
            P(None, COL),
            P(COL, "row"),
            P("row"),
        ),
        out_specs=(P("row", COL), P(None, COL)),
        check_vma=False,
    )
```

profile of v0, /device:TPU:1, one launch (start us, length us, event | category | flops | bytes accessed | tf_op | source)
XLA Modules:
  0.0 435.8 jit_solution(6520451407332182556)
XLA Ops:
  7.3 0.8 add_bitcast_fusion.1
  8.0 0.8 and_or_fusion
  8.8 0.1 broadcast_in_dim.8
  8.9 0.1 reshape.49
  9.1 0.3 broadcast_in_dim.18
  9.4 14.7 %convolution_bitcast_fusion = f32[512,2304]{0,1:T(8,128)} fusion(f32[512,576]{0,1:T(8,128)S(1)} %copy-done, pred[2304,576]{0,1:T(32,128)(4,1)S(1)} %bitcast.21, f32[2304,576]{0,1:T(8,128)} %param.6), kind=kOutput, calls=%fused_computation.1 | convolution fusion | flops 8155054080 | bytes 12533760 | tf_op jit(solution)/shard_map/dot_general | solution.py:58
  24.2 57.5 %reduce-scatter.5.cloned.1.call-done = f32[128,2304]{0,1:T(8,128)} async-done(((f32[512,2304]{0,1:T(8,128)}), f32[128,2304]{0,1:T(8,128)}) %reduce-scatter.5.cloned.1.call-update) | async-done | bytes 1179664 | tf_op jit(solution)/shard_map/reduce_scatter | solution.py:12
  81.7 2.7 copy.34
  84.4 0.0 all-gather.4.cloned.1.call-start
  84.5 35.1 %reduce-scatter.7.cloned.1.call-done = f32[16,2304]{1,0:T(8,128)} async-done(((f32[128,2304]{1,0:T(8,128)}), f32[16,2304]{1,0:T(8,128)}) %reduce-scatter.7.cloned.1.call-update) | async-done | bytes 147472 | tf_op jit(solution)/shard_map/reduce_scatter | solution.py:12
  119.5 1.6 multiply_divide_fusion.1
  121.2 0.2 all-reduce.2.cloned.1.call-start
  121.4 3.3 fusion
  124.7 80.6 %all-gather.4.cloned.1.call-done = f32[512,2304]{1,0:T(8,128)} async-done(((f32[16,2304]{1,0:T(8,128)}), f32[512,2304]{1,0:T(8,128)}) %all-gather.4.cloned.1.call-update) | async-done | bytes 4718608 | tf_op jit(solution)/shard_map/all_gather | solution.py:67
  205.3 13.8 %fusion.1 = f32[512,576]{1,0:T(8,128)S(1)} fusion(f32[512,2304]{1,0:T(8,128)} %all-gather.4.cloned.1.call-done, pred[2304,576]{0,1:T(32,128)(4,1)S(1)} %bitcast.23, f32[2304,576]{0,1:T(8,128)} %param.6), kind=kOutput, calls=%fused_computation.4 | convolution fusion | flops 8155054080 | bytes 12533760 | tf_op jit(solution)/shard_map/dot_general | solution.py:68
  219.1 1.6 reshape.51
  220.7 2.5 pad_maximum_fusion
  223.2 0.4 copy.29
  223.6 66.6 %all-reduce.2.cloned.1.call-done = f32[295488]{0:T(1024)} async-done(((f32[295488]{0:T(1024)}), f32[295488]{0:T(1024)}) %all-reduce.2.cloned.1.call-update) | async-done | bytes 1181968 | tf_op jit(solution)/shard_map/psum | solution.py:20
  290.2 1.3 slice-done
  291.5 1.4 reshape.52
  292.9 1.5 fusion.4
  294.4 1.2 broadcast_subtract_fusion
  295.6 9.3 %all-to-all-start = ((f32[32,16,576]{2,1,0:T(8,128)}), f32[32,16,576]{2,1,0:T(8,128)S(1)}, u32[]{:S(2)}, u32[]{:S(2)}) async-start(f32[32,16,576]{2,1,0:T(8,128)} %bitcast.4), calls=%async_computation.1 | async-start | bytes 2621440 | tf_op jit(solution)/shard_map/all_to_all | solution.py:75
  305.0 27.2 %all-to-all-done = f32[32,16,576]{2,1,0:T(8,128)S(1)} async-done(((f32[32,16,576]{2,1,0:T(8,128)}), f32[32,16,576]{2,1,0:T(8,128)S(1)}, u32[]{:S(2)}, u32[]{:S(2)}) %all-to-all-start) | async-done | bytes 1179680 | tf_op jit(solution)/shard_map/all_to_all | solution.py:75
  332.1 1.5 copy.30
  333.6 1.9 all_to_all.17
  335.5 11.0 %all-gather = f32[64,2304]{1,0:T(8,128)} all-gather(f32[16,2304]{1,0:T(8,128)S(1)} %constant_dynamic-slice_fusion), channel_id=2, replica_groups=mesh['row'=8,'col_0'=4,'col_1'=8] {'col_0'}, dimensions={0}, use_global_device_ids=true | all-gather | bytes 737280 | tf_op jit(solution)/shard_map/all_gather | solution.py:33
  346.5 1.4 copy.32
  347.9 66.0 %all-gather.6.cloned.1.call-done = f32[32,16,2304]{2,1,0:T(8,128)} async-done(((f32[4,16,2304]{2,1,0:T(8,128)}), f32[32,16,2304]{2,1,0:T(8,128)}) %all-gather.6.cloned.1.call-update) | async-done | bytes 4718608 | tf_op jit(solution)/shard_map/all_gather | solution.py:33
  414.0 2.7 copy.31
  416.7 12.6 %convolution_multiply_fusion = f32[2304,576]{0,1:T(8,128)} fusion(f32[512,2304]{1,0:T(8,128)S(1)} %bitcast.24, f32[512,576]{1,0:T(8,128)} %broadcast_subtract_fusion), kind=kOutput, calls=%fused_computation | convolution fusion | flops 8155054080 | bytes 11206656 | tf_op jit(solution)/shard_map/dot_general | solution.py:77
  (23 shorter events, 0.3 us)
Async XLA Ops:
  7.2 2.3 copy-start
  7.2 74.6 %reduce-scatter.5.cloned.1.call-start = ((), (), s32[]{:S(2)}) async-start(), calls=%async_computation.3 | async-start | bytes 5898240 | tf_op jit(solution)/shard_map/reduce_scatter | solution.py:12
  24.2 95.4 %copy-start.2 = (s32[16,2304]{1,0:T(8,128)S(1)}, s32[16,2304]{1,0:T(8,128)}, u32[]{:S(2)}) copy-start(s32[16,2304]{1,0:T(8,128)} %param.10) | copy-start | bytes 442372
  24.2 95.4 %copy-start.3 = (f32[2304]{0:T(1024)S(1)}, f32[2304]{0:T(1024)}, u32[]{:S(2)}) copy-start(f32[2304]{0:T(1024)} %param.11) | copy-start | bytes 27652
  24.2 95.3 %reduce-scatter.7.cloned.1.call-start = ((), (), s32[]{:S(2)}) async-start(), calls=%async_computation.7 | async-start | bytes 1327104 | tf_op jit(solution)/shard_map/reduce_scatter | solution.py:12
  84.4 120.8 %all-gather.4.cloned.1.call-start = ((), (), s32[]{:S(2)}) async-start(), calls=%async_computation.4 | async-start | bytes 4866048 | tf_op jit(solution)/shard_map/all_gather | solution.py:67
  121.2 169.0 %all-reduce.2.cloned.1.call-start = ((), (), s32[]{:S(2)}) async-start(), calls=%async_computation.5 | async-start | bytes 2367488 | tf_op jit(solution)/shard_map/psum | solution.py:20
  220.7 2.5 copy-start.1
  290.2 1.3 slice-start
  291.5 1.4 slice-start.1
  295.6 36.5 %all-to-all-start = ((f32[32,16,576]{2,1,0:T(8,128)}), f32[32,16,576]{2,1,0:T(8,128)S(1)}, u32[]{:S(2)}, u32[]{:S(2)}) async-start(f32[32,16,576]{2,1,0:T(8,128)} %bitcast.4), calls=%async_computation.1 | async-start | bytes 2621440 | tf_op jit(solution)/shard_map/all_to_all | solution.py:75
  304.9 109.1 %all-gather.6.cloned.1.call-start = ((), (), s32[]{:S(2)}) async-start(), calls=%async_computation.6 | async-start | bytes 5308416 | tf_op jit(solution)/shard_map/all_gather | solution.py:33
Sparse Core Ops, SparseCore 0:
  24.3 57.4 reduce-scatter.4
  84.9 34.6 reduce-scatter.6
  122.7 82.5 all-gather.3
  223.3 66.8 all-reduce.1
  346.7 67.2 all-gather.5
where the time goes:
time: 436 us
  waiting for transfers between devices  333 us (76%)
  matrix products  41.1 us (9%)
  local copies, waits for them, and re-layouts  15.4 us (4%)
  between operations  13.9 us (3%)
  other arithmetic  11.6 us (3%)
  blocking collectives  11 us (3%)
  starting transfers between devices  9.69 us (2%)
    reduce_scatter x2, waiting for transfers between devices, own_rows_2(): subtotal = lax.psum_scatter(subtotal, axis, scatter_dimension=0, tiled=True)  92.6 us
    all_gather x1, waiting for transfers between devices, on_device(): fragment = lax.all_gather(ratios, COL, axis=0, tiled=True)  80.6 us
    psum x1, waiting for transfers between devices, in_one(): subtotal = lax.psum(jnp.concatenate([a.ravel() for a in arrays]), axis)  66.6 us
    all_gather x1, waiting for transfers between devices, gather_in_order(): pieces = lax.all_gather(pieces, axes[k], axis=0, tiled=True)  66 us
    all_to_all x1, waiting for transfers between devices, on_device(): lax.all_to_all(centred, COL, split_axis=0, concat_axis=1, tiled=True)  27.2 us
    dot_general x1, matrix products, on_device(): jnp.dot(prior_spectra, masked.T, precision=lax.Precision.HIGHEST, preferr...  14.7 us
    dot_general x1, matrix products, on_device(): jnp.dot(fragment, masked, precision=lax.Precision.HIGHEST, preferred_elem...  13.8 us
    dot_general x1, matrix products, on_device(): jnp.dot(whole_of(own_rows, COL, (0, 1), 0).T, centred, precision=lax.Prec...  12.6 us
  transfers between devices with their start and end apart: 6, of which 6 were waited for; matrix products, arithmetic and copies ran while one was open for 1% of the time, Pallas kernels for 0%

commit v1 on v0

v1 whole, which is shorter than its diff:
```python
import functools

import jax
import jax.numpy as jnp
from jax import lax
from jax.experimental import pallas as pl
from jax.experimental.pallas import tpu as pltpu
from jax.sharding import Mesh
from jax.sharding import PartitionSpec as P

COL = ("col_0", "col_1")
NY, NZ = 4, 8
AXES = {"col_0": NY, "col_1": NZ}
BY_MESH = pl.DeviceIdType.MESH
DIRS = (1, -1)


def wrap(v, n):
    return lax.rem(v + 2 * n, n)


def part_of(direction):
    return 0 if direction == 1 else 1


def greet(devices):
    barrier = pltpu.get_barrier_semaphore()
    for device in devices:
        pl.semaphore_signal(barrier, inc=1, device_id=device, device_id_type=BY_MESH)
    pl.semaphore_wait(barrier, len(devices))


def offset(axis, v):
    return (v, 0) if axis == "col_0" else (0, v)


def plus(a, b):
    return (a[0] + b[0], a[1] + b[1])


def tree():
    stages = []
    for half, (a, b) in enumerate((("col_1", "col_0"), ("col_0", "col_1"))):
        na, nb = AXES[a], AXES[b]

        def onward(axis, direction, shard, step, half=half):
            last = AXES[axis] // 2
            if step >= last:
                return []
            there = plus(shard, offset(axis, -direction))
            return [(half, axis, direction, there, part_of(direction) if step + 1 == last else 2)]

        def branch(shard, half=half, b=b):
            return [(half, b, d, plus(shard, offset(b, -d)), 2) for d in DIRS]

        own = (0, 0)
        stages.append((0, 0, [], [(half, a, d, offset(a, -d), 2) for d in DIRS] + branch(own)))
        for t in range(1, na // 2 + 1):
            if t < na // 2:
                for d in DIRS:
                    key = (half, a, d, offset(a, -d * t), 2)
                    stages.append((t, 1, [key], onward(a, d, key[3], t) + branch(key[3])))
            else:
                keys = [(half, a, d, offset(a, -d * t), part_of(d)) for d in DIRS]
                stages.append((t, 1, keys, branch(offset(a, t))))
        for e in range(-(na // 2) + 1, na // 2 + 1):
            for t in range(1, nb // 2 + 1):
                for d in DIRS:
                    shard = plus(offset(a, e), offset(b, -d * t))
                    key = (half, b, d, shard, 2 if t < nb // 2 else part_of(d))
                    stages.append((abs(e) + t, 2, [key], onward(b, d, shard, t)))
    return stages


def canonical(key):
    half, axis, d, (dy, dz), part = key
    return (half, axis, d, (dy % NY, dz % NZ), part)


STAGES = [
    (r, s, [canonical(k) for k in waits], [canonical(k) for k in starts])
    for r, s, waits, starts in tree()
]
KEYS = sorted({k for _, _, waits, _ in STAGES for k in waits})
INDEX = {k: i for i, k in enumerate(KEYS)}


def columns(part, width):
    return {0: pl.ds(0, width // 2), 1: pl.ds(width // 2, width // 2), 2: pl.ds(0, width)}[part]


class Plane:
    def __init__(self):
        self.y, self.z = lax.axis_index("col_0"), lax.axis_index("col_1")

    def slot(self, shard):
        return wrap(self.y + shard[0], NY) * NZ + wrap(self.z + shard[1], NZ)

    def neighbour(self, axis, d):
        me = self.y if axis == "col_0" else self.z
        return {axis: wrap(me + d, AXES[axis])}

    def greet(self):
        greet([self.neighbour(axis, d) for axis in AXES for d in DIRS])


def gather_kernel(x, out, send, recv):
    plane = Plane()
    width = x.shape[-1]
    plane.greet()

    def copy_in(key):
        half, axis, d, shard, part = key
        here = out.at[plane.slot(shard), half, :, columns(part, width)]
        i = INDEX[key]
        return pltpu.make_async_remote_copy(
            src_ref=here, dst_ref=here, send_sem=send.at[i], recv_sem=recv.at[i],
            device_id=plane.neighbour(axis, -d), device_id_type=BY_MESH,
        )

    def copy_out(key):
        half, axis, d, shard, part = key
        shard = plus(shard, offset(axis, d))
        shard = (shard[0] % NY, shard[1] % NZ)
        cols = columns(part, width)
        there = out.at[plane.slot(shard), half, :, cols]
        src = x.at[half, :, cols] if shard == (0, 0) else there
        i = INDEX[key]
        return pltpu.make_async_remote_copy(
            src_ref=src, dst_ref=there, send_sem=send.at[i], recv_sem=recv.at[i],
            device_id=plane.neighbour(axis, d), device_id_type=BY_MESH,
        )

    started = []
    last = []
    order = sorted(STAGES, key=lambda s: (s[0], s[1]))
    for _, _, waits, starts in order:
        if waits and not starts:
            last.append(waits)
            continue
        for key in waits:
            copy_in(key).wait_recv()
        for key in starts:
            copy = copy_out(key)
            copy.start()
            started.append(copy)
    for half in range(2):
        out[plane.slot((0, 0)), half] = x[half]
    for waits in last:
        for key in waits:
            copy_in(key).wait_recv()
    for copy in started:
        copy.wait_send()


def plane_gather(x, collective_id):
    rows, width = x.shape
    n = len(KEYS)
    out = pl.pallas_call(
        gather_kernel,
        out_shape=jax.ShapeDtypeStruct((NY * NZ, 2, rows // 2, width), x.dtype),
        in_specs=[pl.BlockSpec(memory_space=pltpu.VMEM)],
        out_specs=pl.BlockSpec(memory_space=pltpu.VMEM),
        scratch_shapes=[pltpu.SemaphoreType.DMA((n,)), pltpu.SemaphoreType.DMA((n,))],
        compiler_params=pltpu.CompilerParams(
            collective_id=collective_id, has_side_effects=True, vmem_limit_bytes=48 << 20
        ),
        name="plane_gather",
    )(x.reshape(2, rows // 2, width))
    return out.reshape(NY * NZ * rows, width)


def scatter_kernel(x, out, got, work, send, recv):
    plane = Plane()
    width = x.shape[-1]
    plane.greet()

    def send_of(key, src):
        half, axis, d, shard, part = key
        i = INDEX[key]
        there = got.at[i, :, columns(part, width)]
        return pltpu.make_async_remote_copy(
            src_ref=src, dst_ref=there, send_sem=send.at[i], recv_sem=recv.at[i],
            device_id=plane.neighbour(axis, -d), device_id_type=BY_MESH,
        )

    def recv_of(key):
        half, axis, d, shard, part = key
        i = INDEX[key]
        here = got.at[i, :, columns(part, width)]
        return pltpu.make_async_remote_copy(
            src_ref=here, dst_ref=here, send_sem=send.at[i], recv_sem=recv.at[i],
            device_id=plane.neighbour(axis, d), device_id_type=BY_MESH,
        )

    started = []
    top = max(s[0] for s in STAGES)

    def when(stage):
        r, s, waits, starts = stage
        return (top - r - (0 if starts else 1), 2 - s)

    used = 0
    for r, s, keys, children in sorted(STAGES, key=when):
        half = (keys or children)[0][0]
        if not children:
            for key in keys:
                src = x.at[plane.slot(key[3]), half, :, columns(key[4], width)]
                copy = send_of(key, src)
                copy.start()
                started.append(copy)
            continue
        for child in children:
            recv_of(child).wait_recv()
        shard = keys[0][3] if keys else (0, 0)
        whole = [c for c in children if c[4] == 2]
        split = [c for c in children if c[4] != 2]
        for piece in range(2):
            cols = columns(piece, width)
            total = x[plane.slot(shard), half, :, cols]
            for child in whole + [c for c in split if c[4] == piece]:
                total = total + got[INDEX[child], :, cols]
            if keys:
                work[used, :, cols] = total
            else:
                out[half, :, cols] = total
        if keys:
            for key in keys:
                copy = send_of(key, work.at[used, :, columns(key[4], width)])
                copy.start()
                started.append(copy)
            used += 1
    for copy in started:
        copy.wait_send()


WORKS = sum(1 for _, _, waits, starts in STAGES if waits and starts)


def plane_scatter(x, collective_id):
    rows, width = x.shape
    piece = rows // (NY * NZ * 2)
    n = len(KEYS)
    out = pl.pallas_call(
        scatter_kernel,
        out_shape=jax.ShapeDtypeStruct((2, piece, width), x.dtype),
        in_specs=[pl.BlockSpec(memory_space=pltpu.VMEM)],
        out_specs=pl.BlockSpec(memory_space=pltpu.VMEM),
        scratch_shapes=[
            pltpu.VMEM((n, piece, width), x.dtype),
            pltpu.VMEM((WORKS, piece, width), x.dtype),
            pltpu.SemaphoreType.DMA((n,)),
            pltpu.SemaphoreType.DMA((n,)),
        ],
        compiler_params=pltpu.CompilerParams(
            collective_id=collective_id, has_side_effects=True, vmem_limit_bytes=48 << 20
        ),
        name="plane_scatter",
    )(x.reshape(NY * NZ, 2, piece, width))
    return out.reshape(2 * piece, width)


NX = 4


def row_sum_kernel(g, e, out, eff, met, epart, ehere, acc, got, work, send, recv):
    row = lax.axis_index("row")
    core = lax.rem(row, 2)
    x = lax.div(row, 2)
    other = 1 - core
    partner = {"row": x * 2 + other}

    def at(d):
        return {"row": wrap(x + d, NX) * 2 + core}

    def q(d):
        return wrap(x + d, NX)

    greet([partner, at(1), at(-1), at(2)])
    rows = g.shape[2]
    halves = (pl.ds(0, rows // 2), pl.ds(rows // 2, rows // 2))
    started = []
    ids = {}

    def copy(name, src, dst, device):
        i = ids.setdefault(name, len(ids))
        return pltpu.make_async_remote_copy(
            src_ref=src, dst_ref=dst, send_sem=send.at[i], recv_sem=recv.at[i],
            device_id=device, device_id_type=BY_MESH,
        )

    def go(c):
        c.start()
        started.append(c)

    order = (2, 1, -1, 0)
    for d in order:
        go(copy(("met", d), g.at[other, q(d)], met.at[q(d)], partner))
    go(copy("epart", e, epart.at[0], partner))
    for d in order:
        here = met.at[q(d)]
        copy(("met", d), here, here, partner).wait_recv()
        acc[q(d)] = g[core, q(d)] + met[q(d)]
        if d == 2:
            for s in DIRS:
                h = halves[part_of(s)]
                go(copy(("rs2", s), acc.at[q(2), h], got.at[part_of(s), pl.ds(0, rows // 2)], at(-s)))
        elif d != 0:
            s = -d
            h = halves[part_of(s)]
            dst = got.at[part_of(s), pl.ds(0, rows // 2)]
            copy(("rs2", s), dst, dst, at(s)).wait_recv()
            o = halves[1 - part_of(s)]
            work[part_of(s), h] = acc[q(d), h] + got[part_of(s), pl.ds(0, rows // 2)]
            work[part_of(s), o] = acc[q(d), o]
            go(copy(("rs1", s), work.at[part_of(s)], got.at[2 + part_of(s)], at(-s)))
    copy("epart", e, epart.at[0], partner).wait_recv()
    ehere[...] = e[...] + epart[0]
    for i, d in enumerate((2, 1, -1)):
        go(copy(("e", d), ehere, epart.at[1 + i], at(d)))
    for s in DIRS:
        dst = got.at[2 + part_of(s)]
        copy(("rs1", s), dst, dst, at(s)).wait_recv()
    mine = acc[q(0)] + got[2] + got[3]
    work[2] = mine
    for s in DIRS:
        go(copy(("ag1", s), work.at[2], out.at[core, q(0)], at(s)))
    go(copy(("hand", 0), work.at[2], out.at[core, q(0)], partner))
    out[core, q(0)] = mine
    for s in DIRS:
        block = out.at[core, q(-s)]
        copy(("ag1", s), block, block, at(-s)).wait_recv()
        h = halves[part_of(s)]
        piece = out.at[core, q(-s), h]
        go(copy(("ag2", s), piece, piece, at(s)))
        go(copy(("hand", -s), block, block, partner))
    for s in DIRS:
        piece = out.at[core, q(2), halves[part_of(s)]]
        copy(("ag2", s), piece, piece, at(-s)).wait_recv()
    block = out.at[core, q(2)]
    go(copy(("hand", 2), block, block, partner))
    total = ehere[...]
    for i, d in enumerate((2, 1, -1)):
        copy(("e", d), epart.at[1 + i], epart.at[1 + i], at(-d)).wait_recv()
        total = total + epart[1 + i]
    eff[...] = total
    for d in order:
        block = out.at[other, q(d)]
        copy(("hand", d), block, block, partner).wait_recv()
    for c in started:
        c.wait_send()


def row_sum(g, e, collective_id):
    rows, width = g.shape
    piece = rows // (2 * NX)
    sums, eff = pl.pallas_call(
        row_sum_kernel,
        out_shape=(
            jax.ShapeDtypeStruct((2, NX, piece, width), g.dtype),
            jax.ShapeDtypeStruct(e.shape, e.dtype),
        ),
        in_specs=[pl.BlockSpec(memory_space=pltpu.VMEM)] * 2,
        out_specs=(pl.BlockSpec(memory_space=pltpu.VMEM),) * 2,
        scratch_shapes=[
            pltpu.VMEM((NX, piece, width), g.dtype),
            pltpu.VMEM((4, *e.shape), e.dtype),
            pltpu.VMEM(e.shape, e.dtype),
            pltpu.VMEM((NX, piece, width), g.dtype),
            pltpu.VMEM((4, piece, width), g.dtype),
            pltpu.VMEM((3, piece, width), g.dtype),
            pltpu.SemaphoreType.DMA((20,)),
            pltpu.SemaphoreType.DMA((20,)),
        ],
        compiler_params=pltpu.CompilerParams(
            collective_id=collective_id, has_side_effects=True, vmem_limit_bytes=48 << 20
        ),
        name="row_sum",
    )(g.reshape(2, NX, piece, width), e)
    return sums.reshape(rows, width), eff


def deal_kernel(x, out, send, recv):
    row = lax.axis_index("row")
    core, xx = lax.rem(row, 2), lax.div(row, 2)
    y, z = lax.axis_index("col_0"), lax.axis_index("col_1")
    first = 4 * core
    deals = (y == xx) & (z >= first) & (z < first + 4)
    barrier = pltpu.get_barrier_semaphore()
    targets = [(dy, dz) for dy in range(NY) for dz in range(NZ) if (dy, dz) != (0, 0)]

    def me_at(dy, dz):
        return {"col_0": wrap(y + dy, NY), "col_1": wrap(z + dz, NZ)}

    for k in range(4):
        own = (y == xx) & (z == first + k)

        @pl.when(jnp.logical_not(own))
        def _():
            pl.semaphore_signal(
                barrier, inc=1, device_id={"col_0": xx, "col_1": first + k}, device_id_type=BY_MESH
            )

    @pl.when(deals)
    def _():
        for dy, dz in targets:
            pl.semaphore_signal(barrier, inc=1, device_id=me_at(dy, dz), device_id_type=BY_MESH)
        pl.semaphore_wait(barrier, len(targets) + 3)
        k = wrap(z - first, NZ)
        copies = []
        for i, (dy, dz) in enumerate(targets):
            ty, tz = wrap(y + dy, NY), wrap(z + dz, NZ)
            c = pltpu.make_async_remote_copy(
                src_ref=x.at[ty * NZ + tz], dst_ref=out.at[k], send_sem=send.at[i], recv_sem=recv.at[k],
                device_id={"col_0": ty, "col_1": tz}, device_id_type=BY_MESH,
            )
            c.start()
            copies.append(c)
        out[k] = x[y * NZ + z]
        for c in copies:
            c.wait_send()

    @pl.when(jnp.logical_not(deals))
    def _():
        pl.semaphore_wait(barrier, 4)

    for k in range(4):
        own = (y == xx) & (z == first + k)

        @pl.when(jnp.logical_not(own))
        def _():
            pltpu.make_async_remote_copy(
                src_ref=out.at[k], dst_ref=out.at[k], send_sem=send.at[0], recv_sem=recv.at[k],
                device_id={"col_0": xx, "col_1": first + k}, device_id_type=BY_MESH,
            ).wait_recv()


def deal(x, collective_id):
    rows, width = x.shape
    piece = rows // (NY * NZ)
    out = pl.pallas_call(
        deal_kernel,
        out_shape=jax.ShapeDtypeStruct((4, piece, width), x.dtype),
        in_specs=[pl.BlockSpec(memory_space=pltpu.VMEM)],
        out_specs=pl.BlockSpec(memory_space=pltpu.VMEM),
        scratch_shapes=[pltpu.SemaphoreType.DMA((31,)), pltpu.SemaphoreType.DMA((4,))],
        compiler_params=pltpu.CompilerParams(
            collective_id=collective_id, has_side_effects=True, vmem_limit_bytes=48 << 20
        ),
        name="deal",
    )(x.reshape(NY * NZ, piece, width))
    return jnp.moveaxis(out, 0, 1).reshape(piece, 4 * width)


def on_device(response, tile_map, band_offsets, prior_spectra, boot_counts, spectrum):
    row_place = lax.axis_index("row")
    col_place = lax.axis_index(COL)
    tiles_down, tiles_across = tile_map.shape
    tile_size = response.shape[0] // tiles_down
    measured = row_place * tiles_down + jnp.arange(tiles_down, dtype=jnp.int32)[:, None]
    truth = col_place * tiles_across + jnp.arange(tiles_across, dtype=jnp.int32)[None, :]
    inside = (truth >= measured + band_offsets[:, 0:1]) & (truth <= measured + band_offsets[:, 1:2])
    kept = (truth == measured) | inside & (tile_map == 1)
    expanded = jnp.repeat(jnp.repeat(kept, tile_size, 0), tile_size, 1)
    masked = jnp.where(expanded, response, jnp.zeros_like(response))
    replicas = prior_spectra.shape[0]
    dot = functools.partial(
        lax.dot_general, precision=lax.Precision.HIGH, preferred_element_type=jnp.float32
    )
    part = dot(prior_spectra, masked, (((1,), (1,)), ((), ())))
    folded = plane_scatter(part, 0)
    ratios = boot_counts.astype(jnp.float32) * spectrum[None, :] / folded
    fragment = plane_gather(ratios, 1)
    partial_value = dot(fragment, masked, (((1,), (0,)), ((), ())))
    column_sums = jnp.broadcast_to(jnp.sum(masked, axis=0)[None, :], (8, masked.shape[1]))
    summed, efficiency = row_sum(partial_value, column_sums, 2)
    unfolded = prior_spectra * summed / efficiency[0:1, :]
    centred = unfolded - jnp.mean(unfolded, axis=0)[None, :]
    own_rows = deal(centred, 3)
    covariance = dot(plane_gather(own_rows, 4), centred, (((0,), (0,)), ((), ())))
    return (covariance / (replicas - 1), unfolded)


def solution(mesh):
    torus = Mesh(mesh.devices.reshape(mesh.shape["row"], NY, NZ), ("row", "col_0", "col_1"))
    return jax.shard_map(
        on_device,
        mesh=torus,
        in_specs=(
            P("row", COL),
            P("row", COL),
            P("row", None),
            P(None, COL),
            P(COL, "row"),
            P("row"),
        ),
        out_specs=(P("row", COL), P(None, COL)),
        check_vma=False,
    )
```

time: 436 us -> 192 us (0.44)
  waiting for transfers between devices: 333 us -> 0 us
  Pallas kernels: 0 us -> 159 us
  matrix products: 41.1 us -> 19 us
  between operations: 13.9 us -> 0.82 us
  blocking collectives: 11 us -> 0 us
  local copies, waits for them, and re-layouts: 15.4 us -> 4.59 us
  starting transfers between devices: 9.69 us -> 0 us
  other arithmetic: 11.6 us -> 6.69 us
    pallas_call x0 -> x5, Pallas kernels: none -> 159 us  [the longest x2 79.1 us: plane_gather(): pl.pallas_call(gather_kernel, out_shape=jax.ShapeDtypeStruct((NY * NZ, 2,...]
    all_gather x2 -> x0, waiting for transfers between devices: 147 us -> none  [the longest x1 80.6 us: on_device(): fragment = lax.all_gather(ratios, COL, axis=0, tiled=True)]
    reduce_scatter x2 -> x0, waiting for transfers between devices: 92.6 us -> none  [own_rows_2(): subtotal = lax.psum_scatter(subtotal, axis, scatter_dimension=0, tiled=True)]
    psum x1 -> x0, waiting for transfers between devices: 66.6 us -> none  [in_one(): subtotal = lax.psum(jnp.concatenate([a.ravel() for a in arrays]), axis)]
    all_to_all x1 -> x0, waiting for transfers between devices: 27.2 us -> none  [on_device(): lax.all_to_all(centred, COL, split_axis=0, concat_axis=1, tiled=True)]
    dot_general x3, matrix products: 41.1 us -> 19 us  [the longest x1 6.59 us: on_device(): part = dot(prior_spectra, masked, (((1,), (1,)), ((), ())))]
    all_gather x1 -> x0, blocking collectives: 11 us -> none  [gather_in_order(): pieces = lax.all_gather(pieces, axes[k], axis=0, tiled=True)]
    all_to_all x1 -> x0, starting transfers between devices: 9.31 us -> none  [on_device(): lax.all_to_all(centred, COL, split_axis=0, concat_axis=1, tiled=True)]
  transfers between devices with their start and end apart: 6 -> 0, of which waited for: 6 -> 0; matrix products, arithmetic and copies ran while one was open for 1% -> 0% of each run, Pallas kernels for 0% -> 0%
where the time goes in v1:
time: 192 us; the launch traced here: 190 us
  Pallas kernels  159 us (83%)
  matrix products  19 us (10%)
  other arithmetic  6.69 us (3%)
  local copies, waits for them, and re-layouts  4.59 us (2%)
    pallas_call x2, Pallas kernels, plane_gather(): pl.pallas_call(gather_kernel, out_shape=jax.ShapeDtypeStruct((NY * NZ, 2,...  79.1 us
    pallas_call x1, Pallas kernels, plane_scatter(): pl.pallas_call(scatter_kernel, out_shape=jax.ShapeDtypeStruct((2, piece,...  37.9 us
    pallas_call x1, Pallas kernels, row_sum(): pl.pallas_call(row_sum_kernel, out_shape=(jax.ShapeDtypeStruct((2, NX, pi...  32 us
    pallas_call x1, Pallas kernels, deal(): pl.pallas_call(deal_kernel, out_shape=jax.ShapeDtypeStruct((4, piece, wid...  10 us
    dot_general x1, matrix products, on_device(): part = dot(prior_spectra, masked, (((1,), (1,)), ((), ())))  6.59 us
    dot_general x1, matrix products, on_device(): dot(plane_gather(own_rows, 4), centred, (((0,), (0,)), ((), ())))  6.3 us
    dot_general x1, matrix products, on_device(): partial_value = dot(fragment, masked, (((1,), (0,)), ((), ())))  6.14 us

profile of v1, /device:TPU:1, one launch (start us, length us, event | category | flops | bytes accessed | tf_op | source)
XLA Modules:
  0.0 190.2 jit_solution(2893297567923275784)
XLA Ops:
  0.7 0.8 add_bitcast_fusion.1
  1.4 0.8 and_or_fusion
  2.2 0.1 broadcast_in_dim.8
  2.3 0.1 reshape.51
  2.4 0.3 broadcast_in_dim.9
  2.8 0.0 copy-start
  2.8 0.0 copy-start.1
  2.8 3.4 %select_reduce_fusion = f32[576]{0:T(1024)S(1)} fusion(pred[2304,576]{0,1:T(32,128)(4,1)S(1)} %bitcast.36, f32[2304,576]{0,1:T(8,128)} %param.6), kind=kLoop, calls=%fused_computation.3 | loop fusion | flops 2653632 | bytes 6637824 | tf_op jit(solution)/shard_map/reduce_sum | solution.py:475
  6.3 0.6 copy-done
  6.9 0.3 copy-done.1
  7.2 6.6 %fusion.3 = f32[2304,512]{0,1:T(8,128)S(1)} fusion(f32[512,576]{0,1:T(8,128)S(1)} %copy-done.1, pred[2304,576]{0,1:T(32,128)(4,1)S(1)} %bitcast.37, f32[2304,576]{0,1:T(8,128)S(1)} %copy-done), kind=kOutput, calls=%fused_computation.5 | convolution fusion | flops 4078190592 | bytes 12533760 | tf_op jit(solution)/shard_map/dot_general | solution.py:470
  13.8 0.0 copy-start.3
  13.8 0.0 copy-start.4
  13.8 37.9 %plane_scatter.1 = f32[2,8,2304]{2,1,0:T(8,128)S(1)} custom-call(f32[32,2,8,2304]{3,2,1,0:T(8,128)S(1)} %bitcast.30), custom_call_target="tpu_custom_call" | custom-call | tf_op jit(solution)/shard_map/plane_scatter/pallas_call | solution.py:244
  51.8 0.0 copy-done.3
  51.8 0.0 copy-done.4
  51.8 32.3 %plane_gather.2 = f32[32,2,8,2304]{3,2,1,0:T(8,128)S(1)} custom-call(f32[2,8,2304]{2,1,0:T(8,128)S(1)} %fusion.7.x), custom_call_target="tpu_custom_call" | custom-call | tf_op jit(solution)/shard_map/plane_gather/pallas_call | solution.py:159
  84.2 6.1 %fusion.g = f32[2,4,64,576]{3,2,1,0:T(8,128)S(1)} fusion(f32[2,4,64,2304]{3,2,1,0:T(8,128)S(1)} %bitcast.32, pred[2304,576]{0,1:T(32,128)(4,1)S(1)} %bitcast.38, f32[2304,576]{0,1:T(8,128)S(1)} %copy-done), kind=kOutput, calls=%fused_computation | convolution fusion | flops 4078190592 | bytes 12533760 | tf_op jit(solution)/shard_map/dot_general | solution.py:474
  90.3 32.0 %row_sum.1 = (f32[2,4,64,576]{3,2,1,0:T(8,128)S(1)}, f32[8,576]{1,0:T(8,128)S(1)}) custom-call(f32[2,4,64,576]{3,2,1,0:T(8,128)S(1)} %fusion.g, f32[8,576]{1,0:T(8,128)S(1)} %broadcast_in_dim.22.e), custom_call_target="tpu_custom_call" | custom-call | tf_op jit(solution)/shard_map/row_sum/pallas_call | solution.py:357
  122.3 1.4 copy.8
  123.8 1.5 fusion.10
  125.3 0.0 copy-start.2
  125.3 1.0 copy-done.2
  126.3 0.1 broadcast_subtract_fusion
  126.5 0.4 copy.9
  126.9 10.0 %deal.1 = f32[4,16,576]{2,1,0:T(8,128)S(1)} custom-call(f32[32,16,576]{2,1,0:T(8,128)S(1)} %bitcast.33), custom_call_target="tpu_custom_call" | custom-call | tf_op jit(solution)/shard_map/deal/pallas_call | solution.py:441
  136.9 0.1 copy.10
  137.0 0.1 reshape_reshape.3.x
  137.2 46.7 %plane_gather.3 = f32[32,2,8,2304]{3,2,1,0:T(8,128)S(1)} custom-call(f32[2,8,2304]{2,1,0:T(8,128)S(1)} %reshape_reshape.3.x), custom_call_target="tpu_custom_call" | custom-call | tf_op jit(solution)/shard_map/plane_gather/pallas_call | solution.py:159
  183.9 6.3 %convolution_multiply_fusion = f32[2304,576]{0,1:T(8,128)} fusion(f32[512,2304]{1,0:T(8,128)S(1)} %bitcast.31, f32[512,576]{0,1:T(8,128)S(1)} %broadcast_subtract_fusion), kind=kOutput, calls=%fused_computation.2 | convolution fusion | flops 4078190592 | bytes 11206656 | tf_op jit(solution)/shard_map/dot_general | solution.py:480
  (6 shorter events, 0.1 us)
Async XLA Ops:
  2.8 4.1 %copy-start = (f32[2304,576]{0,1:T(8,128)S(1)}, f32[2304,576]{0,1:T(8,128)}, u32[]{:S(2)}) copy-start(f32[2304,576]{0,1:T(8,128)} %param.6) | copy-start | bytes 15925252
  2.8 4.4 %copy-start.1 = (f32[512,576]{0,1:T(8,128)S(1)}, f32[512,576]{0,1:T(8,128)}, u32[]{:S(2)}) copy-start(f32[512,576]{0,1:T(8,128)} %param.9) | copy-start | bytes 3538948
  13.8 38.0 %copy-start.3 = (s32[16,2304]{1,0:T(8,128)S(1)}, s32[16,2304]{1,0:T(8,128)}, u32[]{:S(2)}) copy-start(s32[16,2304]{1,0:T(8,128)} %param.10) | copy-start | bytes 442372
  13.8 38.0 %copy-start.4 = (f32[2304]{0:T(1024)S(1)}, f32[2304]{0:T(1024)}, u32[]{:S(2)}) copy-start(f32[2304]{0:T(1024)} %param.11) | copy-start | bytes 27652
  125.3 1.0 copy-start.2
